TPU v7x, 256 devices: a whole 4x4x8 slice. The times are simulated.
256 devices in a mesh: space: 64 (over x, z, core), mode: 4 (over y).
Axes of the slice: x: 4, y: 4, z: 8, core: 2. Of those that a mesh axis runs over, the one named last changes fastest.
Arguments:
- modes_in: bfloat16 [120, 131072], P('mode', 'space'), may hold values from -6 to 6
- blocks: bfloat16 [5, 4608, 128, 128], P(None, 'space'), may hold values from -0.25 to 0.25
- block_cols: int32 [1152, 4], P('space'), may hold values from 0 to 15
- send_slot: int32 [16384], P('space'), may hold values from 0 to 511, as said below
- recv_row: int32 [32768], P('space'), may hold values from 0 to 2048, as said below
- mix_cols: int32 [5, 120, 8], replicated, may hold values from 0 to 120, as said below
- mix_coef: float32 [5, 120, 8], replicated, as said below
Outputs:
- first_apply: bfloat16 [120, 131072], P('mode', 'space')
- second_apply: bfloat16 [120, 131072], P('mode', 'space')
Inputs may be any that keep to these rules, and one draw needn't show every extreme that they name: Interface row e of subdomain d goes to subdomain send_slot[d * 256 + e] // 8 at position send_slot[d * 256 + e] % 8. A subdomain's entries are distinct, and for each destination they fill positions from 0 upward, at most 8; one destination, the same for all subdomains, gets 8 rows from every subdomain. `recv_row`: entry o * 64 * 8 + d * 8 + p is the own degree of freedom of subdomain o at which position p from subdomain d is added; it is 2048 exactly where subdomain d sends fewer than p + 1 rows to o. Live entries may repeat. `mix_cols`: column 120 marks a padded slot. Each row of each term has from 4 to 8 live slots, both reached; live columns may repeat. `mix_coef`: zero exactly on padded slots.
All inputs are finite; a program needn't handle non-finite values.
Results may differ from a plain program's by a relative error of at most 0.022.
Values may be sent and summed in bfloat16 or wider, within the bound.
No kernel may reach another device: no remote copies, remote signals or barrier semaphores. Data moves between devices by JAX's collectives and lax.ppermute only.
A program may use at most 64 MiB of HBM per device.

v0:
```python
import jax
import jax.numpy as jnp
from jax import lax
from jax.sharding import PartitionSpec as P


def dense_mixer(mix_cols, mix_coef):
    mode_count = mix_coef.shape[1]
    columns = jnp.arange(mode_count, dtype=jnp.int32)
    onehot_table = (mix_cols[..., None] == columns).astype(jnp.float32)
    return jnp.sum(mix_coef[..., None] * onehot_table, axis=2).astype(jnp.bfloat16)


def block_rows(field_blocks, stiffness, block_cols):
    picked = field_blocks[:, :, block_cols, :]
    return jnp.einsum("mkcnd,kcnde->mce", picked, stiffness, preferred_element_type=jnp.float32)


def local(modes_in, blocks, block_cols, send_slot, recv_row, mix_cols, mix_coef):
    chaos_mixer = dense_mixer(mix_cols, mix_coef)
    term_count = blocks.shape[0]
    block_size = blocks.shape[-1]
    out_blocks, stored = block_cols.shape
    stiffness = blocks.reshape(term_count, out_blocks, stored, block_size, block_size)
    modes_dev, owned_dofs = modes_in.shape
    owned_blocks = owned_dofs // block_size
    slot_total = recv_row.shape[0]

    def send_partials(partials):
        flat_rows = partials.reshape(modes_dev, -1)
        packed = jnp.zeros((modes_dev, slot_total), jnp.float32).at[:, send_slot].set(flat_rows)
        return lax.all_to_all(
            packed.astype(jnp.bfloat16), "space", split_axis=1, concat_axis=1, tiled=True
        ).astype(packed.dtype)

    def mix_field(field_now):
        regrouped = lax.all_to_all(field_now, "mode", split_axis=1, concat_axis=0, tiled=True)
        mixed_all = jnp.einsum(
            "kij,jn->ikn", chaos_mixer, regrouped, preferred_element_type=jnp.float32
        ).astype(jnp.bfloat16)
        return lax.all_to_all(mixed_all, "mode", split_axis=0, concat_axis=2, tiled=True)

    def one_apply(field_now):
        mixed_field = mix_field(field_now)
        field_blocks = mixed_field.reshape(modes_dev, term_count, owned_blocks, block_size)
        products = block_rows(field_blocks, stiffness, block_cols)
        arrived = send_partials(products[:, owned_blocks:])
        owned_part = products[:, :owned_blocks]
        owned_flat = owned_part.reshape(modes_dev, owned_dofs)
        summed = owned_flat.at[:, recv_row].add(arrived, mode="drop")
        return summed.astype(jnp.bfloat16)

    first_apply = one_apply(modes_in)
    second_apply = one_apply(first_apply)
    return (first_apply, second_apply)


def solution(mesh):
    in_specs = (
        P("mode", "space"),
        P(None, "space", None, None),
        P("space", None),
        P("space"),
        P("space"),
        P(),
        P(),
    )
    out_specs = (P("mode", "space"), P("mode", "space"))
    return jax.shard_map(local, mesh=mesh, in_specs=in_specs, out_specs=out_specs, check_vma=False)
```

profile of v0, /device:TPU:1, one launch (start us, length us, event | category | flops | bytes accessed | tf_op | source)
XLA Modules:
  0.0 132.8 jit_solution(6629927610011276790)
XLA Ops:
  0.6 1.0 all_to_all.62
  1.6 0.7 copy.74
  2.3 5.0 %all-to-all-start = ((bf16[30,4,512]{2,0,1:T(8,128)(2,1)}), bf16[30,4,512]{2,0,1:T(8,128)(2,1)S(1)}, u32[]{:S(2)}, u32[]{:S(2)}) async-start(bf16[30,4,512]{2,0,1:T(8,128)(2,1)} %copy.74), calls=%async_computation | async-start | bytes 262144 | tf_op jit(solution)/shard_map/all_to_all | solution.py:37
  7.3 0.9 copy.73
  8.2 0.0 copy-start
  8.2 0.9 copy.72
  9.1 3.5 %select_reduce_fusion = bf16[5,120,120]{2,1,0:T(8,128)(2,1)S(1)} fusion(f32[5,120,8]{2,1,0:T(8,128)S(1)} %copy.73, s32[5,120,8]{2,1,0:T(8,128)S(1)} %copy.72), kind=kLoop, calls=%fused_computation.12 | loop fusion | flops 1656000 | bytes 182400 | tf_op jit(solution)/shard_map/reduce_sum | solution.py:11
  12.6 0.3 fusion.6
  13.0 1.2 copy.75
  14.1 4.2 %all-to-all-start.1 = ((bf16[120,5,512]{2,1,0:T(8,128)(2,1)}), bf16[120,5,512]{2,1,0:T(8,128)(2,1)S(1)}, u32[]{:S(2)}, u32[]{:S(2)}) async-start(bf16[120,5,512]{2,1,0:T(8,128)(2,1)} %copy.75), calls=%async_computation.1 | async-start | bytes 1966080 | tf_op jit(solution)/shard_map/all_to_all | solution.py:41
  18.4 0.1 copy.78
  18.5 0.1 reshape.54
  18.6 12.1 %all-to-all-done.1 = bf16[120,5,512]{2,1,0:T(8,128)(2,1)S(1)} async-done(((bf16[120,5,512]{2,1,0:T(8,128)(2,1)}), bf16[120,5,512]{2,1,0:T(8,128)(2,1)S(1)}, u32[]{:S(2)}, u32[]{:S(2)}) %all-to-all-start.1) | async-done | bytes 614432 | tf_op jit(solution)/shard_map/all_to_all | solution.py:41
  30.7 0.5 copy.77
  31.3 0.2 reshape.43
  31.5 0.2 copy.79
  31.7 2.7 %gather_fusion = bf16[72,30,5,128]{3,1,2,0:T(8,128)(2,1)} fusion(bf16[30,5,16,128]{3,0,2,1:T(8,128)(2,1)S(1)} %copy.79, s32[1024]{0:T(1024)S(1)} %pad_clamp_fusion), kind=kCustom, calls=%fused_computation | custom fusion | bytes 5529888 | tf_op jit(solution)/shard_map/gather | solution.py:15
  34.4 2.9 %copy.80 = bf16[72,30,5,128]{3,0,2,1:T(8,128)(2,1)S(1)} copy(bf16[72,30,5,128]{3,1,2,0:T(8,128)(2,1)} %gather_fusion) | data formatting | bytes 5529600 | tf_op jit(solution)/shard_map/gather | solution.py:15
  37.3 5.4 %fusion.8 = f32[30,18,128]{2,0,1:T(8,128)S(1)} fusion(bf16[5,18,4,128,128]{4,3,2,1,0:T(8,128)(2,1)} %bitcast.85, bf16[30,5,18,4,128]{4,3,2,1,0:T(4,128)(2,1)S(1)} %bitcast.77), kind=kOutput, calls=%fused_computation.18 | convolution fusion | flops 353894400 | bytes 14837760 | tf_op jit(solution)/shard_map/mkcnd,kcnde->mce/dot_general | solution.py:16
  42.8 0.1 copy.85
  43.0 1.2 scatter_custom_fusion
  44.2 0.7 convert_bitcast_fusion.5
  44.9 14.5 %all-to-all-start.2 = ((bf16[30,64,8]{0,2,1:T(8,128)(2,1)}), bf16[30,64,8]{0,2,1:T(8,128)(2,1)S(1)}, u32[]{:S(2)}, u32[]{:S(2)}) async-start(bf16[30,64,8]{0,2,1:T(8,128)(2,1)} %convert_bitcast_fusion.5), calls=%async_computation.2 | async-start | bytes 262144 | tf_op jit(solution)/shard_map/all_to_all | solution.py:32
  59.4 0.4 copy.105
  59.8 10.0 %all-to-all-done.2 = bf16[30,64,8]{0,2,1:T(8,128)(2,1)S(1)} async-done(((bf16[30,64,8]{0,2,1:T(8,128)(2,1)}), bf16[30,64,8]{0,2,1:T(8,128)(2,1)S(1)}, u32[]{:S(2)}, u32[]{:S(2)}) %all-to-all-start.2) | async-done | bytes 30752 | tf_op jit(solution)/shard_map/all_to_all | solution.py:32
  69.7 3.7 %scatter_custom_fusion.1 = f32[30,2048]{0,1:T(8,128)S(1)} fusion(f32[30,2048]{0,1:T(8,128)S(1)} %bitcast.74, s32[512]{0:T(512)S(1)} %compare_select_fusion, bf16[30,64,8]{0,2,1:T(8,128)(2,1)S(1)} %all-to-all-done.2), kind=kCustom, calls=%fused_computation.23 | custom fusion | flops 30720 | bytes 376832 | tf_op jit(solution)/shard_map/scatter-add | solution.py:50
  73.4 0.1 convert_element_type.46
  73.5 0.2 copy.87
  73.7 7.2 %all_to_all.86 = bf16[30,4,512]{2,0,1:T(8,128)(2,1)S(1)} all-to-all(bf16[30,4,512]{2,0,1:T(8,128)(2,1)S(1)} %copy.87), channel_id=1, replica_groups=mesh['space'=64,'mode'=4] {'mode'}, dimensions={1} | all-to-all | bytes 245760 | tf_op jit(solution)/shard_map/all_to_all | solution.py:37
  81.0 0.3 fusion.7
  81.3 0.2 copy.88
  81.5 15.3 %all_to_all.87 = bf16[120,5,512]{2,1,0:T(8,128)(2,1)S(1)} all-to-all(bf16[120,5,512]{2,1,0:T(8,128)(2,1)S(1)} %copy.88), channel_id=1, replica_groups=mesh['space'=64,'mode'=4] {'mode'}, dimensions={0} | all-to-all | bytes 1228800 | tf_op jit(solution)/shard_map/all_to_all | solution.py:41
  96.8 0.5 copy.90
  97.4 0.2 reshape.47
  97.6 0.2 copy.91
  97.8 2.7 %gather_fusion.1 = bf16[72,30,5,128]{3,1,2,0:T(8,128)(2,1)} fusion(bf16[30,5,16,128]{3,0,2,1:T(8,128)(2,1)S(1)} %copy.91, s32[1024]{0:T(1024)S(1)} %pad_clamp_fusion), kind=kCustom, calls=%fused_computation.1 | custom fusion | bytes 5529888 | tf_op jit(solution)/shard_map/gather | solution.py:15
  100.5 2.9 %copy.92 = bf16[72,30,5,128]{3,0,2,1:T(8,128)(2,1)S(1)} copy(bf16[72,30,5,128]{3,1,2,0:T(8,128)(2,1)} %gather_fusion.1) | data formatting | bytes 5529600 | tf_op jit(solution)/shard_map/gather | solution.py:15
  103.4 5.4 %fusion.13 = f32[30,18,128]{2,0,1:T(8,128)S(1)} fusion(bf16[5,18,4,128,128]{4,3,2,1,0:T(8,128)(2,1)} %bitcast.86, bf16[30,5,18,4,128]{4,3,2,1,0:T(4,128)(2,1)S(1)} %bitcast.78), kind=kOutput, calls=%fused_computation.19 | convolution fusion | flops 353894400 | bytes 14837760 | tf_op jit(solution)/shard_map/mkcnd,kcnde->mce/dot_general | solution.py:16
  108.9 0.1 copy.97
  109.0 1.2 scatter_custom_fusion.2
  110.3 0.7 convert_bitcast_fusion.4
  110.9 6.8 %all-to-all-start.5 = ((bf16[30,64,8]{0,2,1:T(8,128)(2,1)}), bf16[30,64,8]{0,2,1:T(8,128)(2,1)S(1)}, u32[]{:S(2)}, u32[]{:S(2)}) async-start(bf16[30,64,8]{0,2,1:T(8,128)(2,1)} %convert_bitcast_fusion.4), calls=%async_computation.5 | async-start | bytes 262144 | tf_op jit(solution)/shard_map/all_to_all | solution.py:32
  117.8 0.9 copy.99
  118.7 0.4 copy.108
  119.1 9.1 %all-to-all-done.5 = bf16[30,64,8]{0,2,1:T(8,128)(2,1)S(1)} async-done(((bf16[30,64,8]{0,2,1:T(8,128)(2,1)}), bf16[30,64,8]{0,2,1:T(8,128)(2,1)S(1)}, u32[]{:S(2)}, u32[]{:S(2)}) %all-to-all-start.5) | async-done | bytes 30752 | tf_op jit(solution)/shard_map/all_to_all | solution.py:32
  128.1 3.7 %scatter_custom_fusion.3 = f32[30,2048]{0,1:T(8,128)S(1)} fusion(f32[30,2048]{0,1:T(8,128)S(1)} %bitcast.73, s32[512]{0:T(512)S(1)} %compare_select_fusion, bf16[30,64,8]{0,2,1:T(8,128)(2,1)S(1)} %all-to-all-done.5), kind=kCustom, calls=%fused_computation.21 | custom fusion | flops 30720 | bytes 376832 | tf_op jit(solution)/shard_map/scatter-add | solution.py:50
  131.8 0.1 convert_element_type.52
  131.9 0.9 copy.100
  (22 shorter events, 0.2 us)
Async XLA Ops:
  2.3 10.3 %all-to-all-start = ((bf16[30,4,512]{2,0,1:T(8,128)(2,1)}), bf16[30,4,512]{2,0,1:T(8,128)(2,1)S(1)}, u32[]{:S(2)}, u32[]{:S(2)}) async-start(bf16[30,4,512]{2,0,1:T(8,128)(2,1)} %copy.74), calls=%async_computation | async-start | bytes 262144 | tf_op jit(solution)/shard_map/all_to_all | solution.py:37
  8.2 10.2 %copy-start = (s32[18,4]{0,1:T(4,128)S(1)}, s32[18,4]{0,1:T(4,128)}, u32[]{:S(2)}) copy-start(s32[18,4]{0,1:T(4,128)} %param.9) | copy-start | bytes 868
  8.2 10.4 %copy-start.2 = (s32[256]{0:T(256)S(1)}, s32[256]{0:T(256)}, u32[]{:S(2)}) copy-start(s32[256]{0:T(256)} %param.10) | copy-start | bytes 3076
  14.1 16.6 %all-to-all-start.1 = ((bf16[120,5,512]{2,1,0:T(8,128)(2,1)}), bf16[120,5,512]{2,1,0:T(8,128)(2,1)S(1)}, u32[]{:S(2)}, u32[]{:S(2)}) async-start(bf16[120,5,512]{2,1,0:T(8,128)(2,1)} %copy.75), calls=%async_computation.1 | async-start | bytes 1966080 | tf_op jit(solution)/shard_map/all_to_all | solution.py:41
  37.3 22.0 %copy-start.1 = (s32[512]{0:T(512)S(1)}, s32[512]{0:T(512)}, u32[]{:S(2)}) copy-start(s32[512]{0:T(512)} %param.11) | copy-start | bytes 6148
  44.9 24.9 %all-to-all-start.2 = ((bf16[30,64,8]{0,2,1:T(8,128)(2,1)}), bf16[30,64,8]{0,2,1:T(8,128)(2,1)S(1)}, u32[]{:S(2)}, u32[]{:S(2)}) async-start(bf16[30,64,8]{0,2,1:T(8,128)(2,1)} %convert_bitcast_fusion.5), calls=%async_computation.2 | async-start | bytes 262144 | tf_op jit(solution)/shard_map/all_to_all | solution.py:32
  110.9 17.2 %all-to-all-start.5 = ((bf16[30,64,8]{0,2,1:T(8,128)(2,1)}), bf16[30,64,8]{0,2,1:T(8,128)(2,1)S(1)}, u32[]{:S(2)}, u32[]{:S(2)}) async-start(bf16[30,64,8]{0,2,1:T(8,128)(2,1)} %convert_bitcast_fusion.4), calls=%async_computation.5 | async-start | bytes 262144 | tf_op jit(solution)/shard_map/all_to_all | solution.py:32
where the time goes:
time: 133 us
  waiting for transfers between devices  31.1 us (23%)
  starting transfers between devices  30.6 us (23%)
  local copies, waits for them, and re-layouts  23.9 us (18%)
  blocking collectives  22.5 us (17%)
  other arithmetic  12.3 us (9%)
  matrix products  11.4 us (9%)
    all_to_all x2, starting transfers between devices, send_partials(): lax.all_to_all(packed.astype(jnp.bfloat16), 'space', split_axis=1, concat...  21.3 us
    all_to_all x2, waiting for transfers between devices, send_partials(): lax.all_to_all(packed.astype(jnp.bfloat16), 'space', split_axis=1, concat...  19 us
    all_to_all x1, blocking collectives, mix_field(): lax.all_to_all(mixed_all, 'mode', split_axis=0, concat_axis=2, tiled=True)  15.3 us
    all_to_all x1, waiting for transfers between devices, mix_field(): lax.all_to_all(mixed_all, 'mode', split_axis=0, concat_axis=2, tiled=True)  12.1 us
    gather x4, local copies, waits for them, and re-layouts, block_rows(): picked = field_blocks[:, :, block_cols, :]  11.3 us
    dot_general x2, matrix products, block_rows(): jnp.einsum('mkcnd,kcnde->mce', picked, stiffness, preferred_element_type=...  10.8 us
    scatter-add x2, other arithmetic, one_apply(): summed = owned_flat.at[:, recv_row].add(arrived, mode='drop')  7.39 us
    all_to_all x1, blocking collectives, mix_field(): lax.all_to_all(field_now, 'mode', split_axis=1, concat_axis=0, tiled=True)  7.22 us
  transfers between devices with their start and end apart: 4, of which 3 were waited for; matrix products, arithmetic and copies ran while one was open for 5% of the time, Pallas kernels for 0%

commit v1 on v0

--- a/solution.py
+++ b/solution.py
@@ -2,6 +2,13 @@
 import jax.numpy as jnp
 from jax import lax
 from jax.sharding import PartitionSpec as P
+
+
+def swap_blocks(x, axis, split, join):
+    n_dev = lax.axis_size(axis)
+    blocks = jnp.stack(jnp.split(x, n_dev, axis=split), axis=0)
+    blocks = lax.all_to_all(blocks, axis, split_axis=0, concat_axis=0)
+    return jnp.concatenate(blocks, axis=join)
 
 
 def dense_mixer(mix_cols, mix_coef):
@@ -38,7 +45,7 @@
         mixed_all = jnp.einsum(
             "kij,jn->ikn", chaos_mixer, regrouped, preferred_element_type=jnp.float32
         ).astype(jnp.bfloat16)
-        return lax.all_to_all(mixed_all, "mode", split_axis=0, concat_axis=2, tiled=True)
+        return swap_blocks(mixed_all, "mode", 0, 2)
 
     def one_apply(field_now):
         mixed_field = mix_field(field_now)

time: 133 us -> 126 us (0.947)
  waiting for transfers between devices: 31.1 us -> 27.3 us
  blocking collectives: 22.5 us -> 18.9 us
    all_to_all x1, waiting for transfers between devices: 12.1 us -> 8.3 us  [swap_blocks(): blocks = lax.all_to_all(blocks, axis, split_axis=0, concat_axis=0)]
    all_to_all x1, blocking collectives: 15.3 us -> 11.7 us  [swap_blocks(): blocks = lax.all_to_all(blocks, axis, split_axis=0, concat_axis=0)]
    convert_element_type x2 -> x0, local copies, waits for them, and re-layouts: 1.42 us -> none  [mix_field(): mixed_all = jnp.einsum('kij,jn->ikn', chaos_mixer, regrouped, preferred_e...]
  transfers between devices with their start and end apart: 4 -> 4, of which waited for: 3 -> 3; matrix products, arithmetic and copies ran while one was open for 5% -> 6% of each run, Pallas kernels for 0% -> 0%
where the time goes in v1:
time: 126 us
  starting transfers between devices  31 us (25%)
  waiting for transfers between devices  27.3 us (22%)
  local copies, waits for them, and re-layouts  22.6 us (18%)
  blocking collectives  18.9 us (15%)
  other arithmetic  13.4 us (11%)
  matrix products  11.4 us (9%)
    all_to_all x2, starting transfers between devices, send_partials(): lax.all_to_all(packed.astype(jnp.bfloat16), 'space', split_axis=1, concat...  21.7 us
    all_to_all x2, waiting for transfers between devices, send_partials(): lax.all_to_all(packed.astype(jnp.bfloat16), 'space', split_axis=1, concat...  19 us
    all_to_all x1, blocking collectives, swap_blocks(): blocks = lax.all_to_all(blocks, axis, split_axis=0, concat_axis=0)  11.7 us
    gather x4, local copies, waits for them, and re-layouts, block_rows(): picked = field_blocks[:, :, block_cols, :]  11.3 us
    dot_general x2, matrix products, block_rows(): jnp.einsum('mkcnd,kcnde->mce', picked, stiffness, preferred_element_type=...  10.8 us
    all_to_all x1, waiting for transfers between devices, swap_blocks(): blocks = lax.all_to_all(blocks, axis, split_axis=0, concat_axis=0)  8.3 us
    scatter-add x2, other arithmetic, one_apply(): summed = owned_flat.at[:, recv_row].add(arrived, mode='drop')  7.39 us
    all_to_all x1, blocking collectives, mix_field(): lax.all_to_all(field_now, 'mode', split_axis=1, concat_axis=0, tiled=True)  7.22 us
  transfers between devices with their start and end apart: 4, of which 3 were waited for; matrix products, arithmetic and copies ran while one was open for 6% of the time, Pallas kernels for 0%

profile of v1, /device:TPU:1, one launch (start us, length us, event | category | flops | bytes accessed | tf_op | source)
XLA Modules:
  0.0 125.6 jit_solution(15763148590981107466)
XLA Ops:
  0.6 1.0 all_to_all.46
  1.6 0.7 copy.45
  2.3 5.0 %all-to-all-start = ((bf16[30,4,512]{2,0,1:T(8,128)(2,1)}), bf16[30,4,512]{2,0,1:T(8,128)(2,1)S(1)}, u32[]{:S(2)}, u32[]{:S(2)}) async-start(bf16[30,4,512]{2,0,1:T(8,128)(2,1)} %copy.45), calls=%async_computation | async-start | bytes 262144 | tf_op jit(solution)/shard_map/all_to_all | solution.py:44
  7.3 0.9 copy.44
  8.2 0.9 copy.43
  9.1 3.5 %select_reduce_fusion = bf16[5,120,120]{2,1,0:T(8,128)(2,1)S(1)} fusion(f32[5,120,8]{2,1,0:T(8,128)S(1)} %copy.44, s32[5,120,8]{2,1,0:T(8,128)S(1)} %copy.43), kind=kLoop, calls=%fused_computation.12 | loop fusion | flops 1656000 | bytes 182400 | tf_op jit(solution)/shard_map/reduce_sum | solution.py:18
  12.6 0.3 fusion.6
  12.9 0.1 slice_bitcast_fusion.7
  13.1 0.9 pad_maximum_fusion
  14.0 4.2 %all-to-all-start.1 = ((bf16[4,30,5,512]{3,1,2,0:T(8,128)(2,1)}), bf16[4,30,5,512]{3,1,2,0:T(8,128)(2,1)S(1)}, u32[]{:S(2)}, u32[]{:S(2)}) async-start(bf16[4,30,5,512]{3,1,2,0:T(8,128)(2,1)} %pad_maximum_fusion), calls=%async_computation.1 | async-start | bytes 1310720 | tf_op jit(solution)/shard_map/all_to_all | solution.py:10
  18.3 0.1 copy.47
  18.4 0.1 reshape.52
  18.5 8.3 %all-to-all-done.1 = bf16[4,30,5,512]{3,1,2,0:T(8,128)(2,1)S(1)} async-done(((bf16[4,30,5,512]{3,1,2,0:T(8,128)(2,1)}), bf16[4,30,5,512]{3,1,2,0:T(8,128)(2,1)S(1)}, u32[]{:S(2)}, u32[]{:S(2)}) %all-to-all-start.1) | async-done | bytes 614432 | tf_op jit(solution)/shard_map/all_to_all | solution.py:10
  26.8 0.5 copy.46
  27.3 0.2 reshape_reshape.6
  27.5 0.2 copy.48
  27.7 2.7 %gather_fusion = bf16[72,30,5,128]{3,1,2,0:T(8,128)(2,1)} fusion(bf16[30,5,16,128]{3,0,2,1:T(8,128)(2,1)S(1)} %copy.48, s32[1024]{0:T(1024)S(1)} %pad_clamp_fusion), kind=kCustom, calls=%fused_computation | custom fusion | bytes 5529888 | tf_op jit(solution)/shard_map/gather | solution.py:22
  30.5 2.9 %copy.49 = bf16[72,30,5,128]{3,0,2,1:T(8,128)(2,1)S(1)} copy(bf16[72,30,5,128]{3,1,2,0:T(8,128)(2,1)} %gather_fusion) | data formatting | bytes 5529600 | tf_op jit(solution)/shard_map/gather | solution.py:22
  33.4 5.4 %fusion.8 = f32[30,18,128]{2,0,1:T(8,128)S(1)} fusion(bf16[5,18,4,128,128]{4,3,2,1,0:T(8,128)(2,1)} %bitcast.95, bf16[30,5,18,4,128]{4,3,2,1,0:T(4,128)(2,1)S(1)} %bitcast.85), kind=kOutput, calls=%fused_computation.18 | convolution fusion | flops 353894400 | bytes 14837760 | tf_op jit(solution)/shard_map/mkcnd,kcnde->mce/dot_general | solution.py:23
  38.9 0.1 copy.54
  39.0 1.2 scatter_custom_fusion
  40.2 0.7 convert_bitcast_fusion.5
  40.9 14.8 %all-to-all-start.2 = ((bf16[30,64,8]{0,2,1:T(8,128)(2,1)}), bf16[30,64,8]{0,2,1:T(8,128)(2,1)S(1)}, u32[]{:S(2)}, u32[]{:S(2)}) async-start(bf16[30,64,8]{0,2,1:T(8,128)(2,1)} %convert_bitcast_fusion.5), calls=%async_computation.2 | async-start | bytes 262144 | tf_op jit(solution)/shard_map/all_to_all | solution.py:39
  55.7 0.4 copy.70
  56.1 10.0 %all-to-all-done.2 = bf16[30,64,8]{0,2,1:T(8,128)(2,1)S(1)} async-done(((bf16[30,64,8]{0,2,1:T(8,128)(2,1)}), bf16[30,64,8]{0,2,1:T(8,128)(2,1)S(1)}, u32[]{:S(2)}, u32[]{:S(2)}) %all-to-all-start.2) | async-done | bytes 30752 | tf_op jit(solution)/shard_map/all_to_all | solution.py:39
  66.0 3.7 %scatter_custom_fusion.1 = f32[30,2048]{0,1:T(8,128)S(1)} fusion(f32[30,2048]{0,1:T(8,128)S(1)} %bitcast.84, s32[512]{0:T(512)S(1)} %compare_select_fusion, bf16[30,64,8]{0,2,1:T(8,128)(2,1)S(1)} %all-to-all-done.2), kind=kCustom, calls=%fused_computation.25 | custom fusion | flops 30720 | bytes 376832 | tf_op jit(solution)/shard_map/scatter-add | solution.py:57
  69.8 0.2 copy.56
  70.0 7.2 %all_to_all.66 = bf16[30,4,512]{2,0,1:T(8,128)(2,1)S(1)} all-to-all(bf16[30,4,512]{2,0,1:T(8,128)(2,1)S(1)} %copy.56), channel_id=1, replica_groups=mesh['space'=64,'mode'=4] {'mode'}, dimensions={1} | all-to-all | bytes 245760 | tf_op jit(solution)/shard_map/all_to_all | solution.py:44
  77.3 0.3 fusion.7
  77.6 0.1 slice_bitcast_fusion.3
  77.8 0.1 pad_maximum_fusion.1
  77.9 11.7 %all_to_all.67 = bf16[4,30,5,512]{3,1,2,0:T(8,128)(2,1)S(1)} all-to-all(bf16[4,30,5,512]{3,1,2,0:T(8,128)(2,1)S(1)} %pad_maximum_fusion.1), channel_id=1, replica_groups=mesh['space'=64,'mode'=4] {'mode'}, dimensions={0} | all-to-all | bytes 1228800 | tf_op jit(solution)/shard_map/all_to_all | solution.py:10
  89.6 0.5 copy.57
  90.0 0.2 reshape_reshape.7
  90.3 0.2 copy.58
  90.5 2.7 %gather_fusion.1 = bf16[72,30,5,128]{3,1,2,0:T(8,128)(2,1)} fusion(bf16[30,5,16,128]{3,0,2,1:T(8,128)(2,1)S(1)} %copy.58, s32[1024]{0:T(1024)S(1)} %pad_clamp_fusion), kind=kCustom, calls=%fused_computation.1 | custom fusion | bytes 5529888 | tf_op jit(solution)/shard_map/gather | solution.py:22
  93.2 2.9 %copy.59 = bf16[72,30,5,128]{3,0,2,1:T(8,128)(2,1)S(1)} copy(bf16[72,30,5,128]{3,1,2,0:T(8,128)(2,1)} %gather_fusion.1) | data formatting | bytes 5529600 | tf_op jit(solution)/shard_map/gather | solution.py:22
  96.1 5.4 %fusion.13 = f32[30,18,128]{2,0,1:T(8,128)S(1)} fusion(bf16[5,18,4,128,128]{4,3,2,1,0:T(8,128)(2,1)} %bitcast.96, bf16[30,5,18,4,128]{4,3,2,1,0:T(4,128)(2,1)S(1)} %bitcast.86), kind=kOutput, calls=%fused_computation.19 | convolution fusion | flops 353894400 | bytes 14837760 | tf_op jit(solution)/shard_map/mkcnd,kcnde->mce/dot_general | solution.py:23
  101.6 0.1 copy.64
  101.7 1.2 scatter_custom_fusion.2
  102.9 0.7 convert_bitcast_fusion.4
  103.6 6.9 %all-to-all-start.5 = ((bf16[30,64,8]{0,2,1:T(8,128)(2,1)}), bf16[30,64,8]{0,2,1:T(8,128)(2,1)S(1)}, u32[]{:S(2)}, u32[]{:S(2)}) async-start(bf16[30,64,8]{0,2,1:T(8,128)(2,1)} %convert_bitcast_fusion.4), calls=%async_computation.5 | async-start | bytes 262144 | tf_op jit(solution)/shard_map/all_to_all | solution.py:39
  110.5 0.9 copy.66
  111.5 0.4 copy.71
  111.8 9.1 %all-to-all-done.5 = bf16[30,64,8]{0,2,1:T(8,128)(2,1)S(1)} async-done(((bf16[30,64,8]{0,2,1:T(8,128)(2,1)}), bf16[30,64,8]{0,2,1:T(8,128)(2,1)S(1)}, u32[]{:S(2)}, u32[]{:S(2)}) %all-to-all-start.5) | async-done | bytes 30752 | tf_op jit(solution)/shard_map/all_to_all | solution.py:39
  120.9 3.7 %scatter_custom_fusion.3 = f32[30,2048]{0,1:T(8,128)S(1)} fusion(f32[30,2048]{0,1:T(8,128)S(1)} %bitcast.83, s32[512]{0:T(512)S(1)} %compare_select_fusion, bf16[30,64,8]{0,2,1:T(8,128)(2,1)S(1)} %all-to-all-done.5), kind=kCustom, calls=%fused_computation.23 | custom fusion | flops 30720 | bytes 376832 | tf_op jit(solution)/shard_map/scatter-add | solution.py:57
  124.6 0.1 convert_element_type.52
  124.7 0.9 copy.67
  (24 shorter events, 0.3 us)
Async XLA Ops:
  2.3 10.3 %all-to-all-start = ((bf16[30,4,512]{2,0,1:T(8,128)(2,1)}), bf16[30,4,512]{2,0,1:T(8,128)(2,1)S(1)}, u32[]{:S(2)}, u32[]{:S(2)}) async-start(bf16[30,4,512]{2,0,1:T(8,128)(2,1)} %copy.45), calls=%async_computation | async-start | bytes 262144 | tf_op jit(solution)/shard_map/all_to_all | solution.py:44
  9.1 9.2 %copy-start = (s32[18,4]{0,1:T(4,128)S(1)}, s32[18,4]{0,1:T(4,128)}, u32[]{:S(2)}) copy-start(s32[18,4]{0,1:T(4,128)} %param.9) | copy-start | bytes 868
  9.1 9.4 %copy-start.2 = (s32[256]{0:T(256)S(1)}, s32[256]{0:T(256)}, u32[]{:S(2)}) copy-start(s32[256]{0:T(256)} %param.10) | copy-start | bytes 3076
  14.0 12.8 %all-to-all-start.1 = ((bf16[4,30,5,512]{3,1,2,0:T(8,128)(2,1)}), bf16[4,30,5,512]{3,1,2,0:T(8,128)(2,1)S(1)}, u32[]{:S(2)}, u32[]{:S(2)}) async-start(bf16[4,30,5,512]{3,1,2,0:T(8,128)(2,1)} %pad_maximum_fusion), calls=%async_computation.1 | async-start | bytes 1310720 | tf_op jit(solution)/shard_map/all_to_all | solution.py:10
  33.4 22.3 %copy-start.1 = (s32[512]{0:T(512)S(1)}, s32[512]{0:T(512)}, u32[]{:S(2)}) copy-start(s32[512]{0:T(512)} %param.11) | copy-start | bytes 6148
  40.9 25.2 %all-to-all-start.2 = ((bf16[30,64,8]{0,2,1:T(8,128)(2,1)}), bf16[30,64,8]{0,2,1:T(8,128)(2,1)S(1)}, u32[]{:S(2)}, u32[]{:S(2)}) async-start(bf16[30,64,8]{0,2,1:T(8,128)(2,1)} %convert_bitcast_fusion.5), calls=%async_computation.2 | async-start | bytes 262144 | tf_op jit(solution)/shard_map/all_to_all | solution.py:39
  103.6 17.3 %all-to-all-start.5 = ((bf16[30,64,8]{0,2,1:T(8,128)(2,1)}), bf16[30,64,8]{0,2,1:T(8,128)(2,1)S(1)}, u32[]{:S(2)}, u32[]{:S(2)}) async-start(bf16[30,64,8]{0,2,1:T(8,128)(2,1)} %convert_bitcast_fusion.4), calls=%async_computation.5 | async-start | bytes 262144 | tf_op jit(solution)/shard_map/all_to_all | solution.py:39
